TPU v7x, 32 devices: a whole 2x2x4 slice. The times are simulated.
32 devices in a mesh: ctx: 8 (over y, x, core), head: 4 (over z).
Axes of the slice: x: 2, y: 2, z: 4, core: 2. Of those that a mesh axis runs over, the one named last changes fastest.
Arguments:
- query_key: bfloat16 [4096, 1024], P('ctx', 'head'), may hold values from -6 to 6
- values: bfloat16 [4096, 4096], P('ctx', 'head'), may hold values from -6 to 6
- out_grad: bfloat16 [4096, 4096], P('ctx', 'head'), may hold values from -6 to 6
- out_weight: bfloat16 [4096, 4096], P('head'), may hold values from -0.09375 to 0.09375
- doc_lengths: int32 [32], replicated, may hold values from 1 to 2048, 4096 in all
Outputs:
- qk_grad: bfloat16 [4096, 1024], P('ctx', 'head')
- value_grad: bfloat16 [4096, 4096], P('ctx', 'head')
- proj_grad: float32 [4096, 4096], P('head', 'ctx')
Inputs may be any that keep to these rules, and one draw needn't show every extreme that they name: `doc_lengths`: the documents fill all 4096 positions in order; the longest has exactly 2048 tokens.
All inputs are finite; a program needn't handle non-finite values.
Results may differ from a plain program's by a relative error of at most 0.0068.
Values may be sent and summed in bfloat16 or wider, within the bound.
A program may use at most 128 MiB of HBM per device.

v0:
```python
import functools
import math

import jax
import jax.numpy as jnp
import numpy as np
from jax import lax
from jax.experimental import pallas as pl
from jax.experimental.pallas import tpu as pltpu
from jax.sharding import PartitionSpec as P

HEAD = 128
QK = 16
DOC_MOST = 2048

quad_scale = 0.25 / math.sqrt(2.0)

bf16 = jnp.bfloat16
f32 = jnp.float32
MESH = pl.DeviceIdType.MESH

PAIRS = [(a, b) for a in range(QK) for b in range(a, QK)]
FEAT = 160


def tables():
    left = np.zeros((FEAT, QK), np.float32)
    right = np.zeros((FEAT, QK), np.float32)
    cols = np.zeros((FEAT, 4), np.float32)
    cols[0, 0] = cols[0, 1] = cols[0, 2] = 1.0
    cols[:, 3] = 1.0
    for a in range(QK):
        left[1 + a, a] = 1.0
        cols[1 + a, 1] = 1.0
        cols[1 + a, 2] = 0.5
    for place, (a, b) in enumerate(PAIRS):
        left[1 + QK + place, a] = 1.0
        right[1 + QK + place, b] = 1.0
        cols[1 + QK + place, 2] = quad_scale
        cols[1 + QK + place, 3] = 1.0 if a == b else 2.0
    return left, right, cols


LEFT, RIGHT, COLS = tables()


def mm(a, b, ca, cb):
    return lax.dot_general(a, b, (((ca,), (cb,)), ((), ())), preferred_element_type=f32)


def split_rows(rows):
    high = rows.astype(bf16).astype(f32)
    place = lax.broadcasted_iota(jnp.int32, rows.shape, 0)
    return jnp.where(place == 0, high, jnp.where(place == 1, rows - high, 0.0)).astype(bf16)


def kernel(
    count,
    depth,
    docs_ref,
    qk_ref,
    v_ref,
    g_ref,
    w_ref,
    lcol_ref,
    rcol_ref,
    lrow_ref,
    rrow_ref,
    cols_ref,
    wrow_ref,
    qk_out,
    v_out,
    p_out,
    out_ref,
    wbuf,
    qkt,
    qkg,
    phiq,
    phik,
    mask_ref,
    wb_ref,
    y_ref,
    att_ref,
    up_ref,
    ng_ref,
    den_ref,
    dg_ref,
    rows_ref,
    st_ref,
    nin_ref,
    own,
    oth,
    pair,
    arr,
    nown,
    noth,
    npair,
    narr,
    vg_ref,
    acc,
    psend,
    precv,
    rbuf,
    pbuf,
    wsem,
    gsem,
    osem,
    ag_send,
    ag_recv,
    c_send,
    c_recv,
    p_ssem,
    p_rsem,
    s_ssem,
    s_rsem,
):
    tokens = qk_ref.shape[0]
    heads = v_ref.shape[1] // HEAD
    rows_all = heads * HEAD
    shard = g_ref.shape[1]
    chips = count // 2
    bits = chips.bit_length() - 1
    roots = chips // depth
    cw = shard // (2 * roots)
    half_t = tokens // 2
    half_r = rows_all // 2
    span = arr.shape[1]
    c = lax.axis_index("ctx")
    z = lax.axis_index("head")
    chip = c // 2
    core = c % 2
    other_core = 1 - core
    partner = 2 * chip + other_core
    chip_bit = [(chip // (1 << b)) % 2 for b in range(bits)]
    neighbour = [2 * (chip + (1 - 2 * chip_bit[b]) * (1 << b)) + core for b in range(bits)]

    barrier = pltpu.get_barrier_semaphore()

    met = [(None, {"ctx": partner, "head": z})]
    met += [(z > 0, {"ctx": c, "head": z - 1}), (z < depth - 1, {"ctx": c, "head": z + 1})]
    met += [(None, {"ctx": neighbour[b], "head": z}) for b in range(bits) if (1 << b) > span]
    for k in range(1, span + 1):
        met += [
            (chip >= k, {"ctx": c - 2 * k, "head": z}),
            (chip + k < chips, {"ctx": c + 2 * k, "head": z}),
        ]
    peers = 0
    for cond, where in met:

        def greet(where=where):
            pl.semaphore_signal(barrier, inc=1, device_id=where, device_id_type=MESH)

        if cond is None:
            greet()
            peers = peers + 1
        else:
            pl.when(cond)(greet)
            peers = peers + cond.astype(jnp.int32)
    pl.semaphore_wait(barrier, peers)

    def piece(n):
        if n == 0:
            return z
        k = (n + 1) // 2
        inner = z - k if n % 2 else z + k
        low_side = 1 - (2 * z + 1) // depth
        lesser = low_side * z + (1 - low_side) * (depth - 1 - z)
        outer = low_side * n + (1 - low_side) * (depth - 1 - n)
        beyond = (n - 2 * lesser - 1 + 4 * depth) // (4 * depth)
        return (1 - beyond) * inner + beyond * outer

    def slot(way, k, level):
        if k == 0:
            return 0
        low_side = 1 - (2 * level + 1) // depth
        lesser = low_side * level + (1 - low_side) * (depth - 1 - level)
        beyond = (k - lesser - 1 + 2 * depth) // (2 * depth)
        return (1 - beyond) * (2 * k - 1 + way) + beyond * (lesser + k)

    def part_rows(part):
        return pl.ds(part * half_t, half_t)

    def ag(way, k, part):
        to = z + 1 - 2 * way
        if k == 0:
            src = g_ref.at[part_rows(part), :]
        else:
            src = out_ref.at[slot(way, k, z), part_rows(part), :]
        return pltpu.make_async_remote_copy(
            src_ref=src,
            dst_ref=out_ref.at[slot(way, k + 1, to), part_rows(part), :],
            send_sem=ag_send.at[way, k, part],
            recv_sem=ag_recv.at[way, k, part],
            device_id={"ctx": c, "head": to},
            device_id_type=MESH,
        )

    def ag_arrival(way, k, part):
        came = out_ref.at[slot(way, k, z), part_rows(part), :]
        return pltpu.make_async_remote_copy(
            src_ref=came,
            dst_ref=came,
            send_sem=ag_send.at[way, k, part],
            recv_sem=ag_recv.at[way, k - 1, part],
            device_id={"ctx": c, "head": z - 1 + 2 * way},
            device_id_type=MESH,
        )

    def ag_cond(way, k):
        if way == 0:
            return (z >= k) & (z < depth - 1)
        return (z + k <= depth - 1) & (z > 0)

    def ag_has(way, k):
        return z >= k if way == 0 else z + k <= depth - 1

    for part in range(2):
        for way in range(2):
            pl.when(ag_cond(way, 0))(lambda way=way, part=part: ag(way, 0, part).start())

    def arrive(k, part):
        for way in range(2):

            @pl.when(ag_has(way, k))
            def _(way=way):
                ag_arrival(way, k, part).wait_recv()

            if k < depth - 1:
                pl.when(ag_cond(way, k))(lambda way=way: ag(way, k, part).start())

    own_copy = pltpu.make_async_copy(g_ref, out_ref.at[0], gsem)
    own_copy.start()

    def w_copy(n):
        at = pl.multiple_of(piece(n) * shard, shard)
        return pltpu.make_async_copy(w_ref.at[:, pl.ds(at, shard)], wbuf.at[n % 2], wsem.at[n % 2])

    w_copy(0).start()
    if depth > 1:
        w_copy(1).start()

    places_row = c * tokens + lax.broadcasted_iota(jnp.int32, (1, tokens), 1)
    places_col = c * tokens + lax.broadcasted_iota(jnp.int32, (tokens, 1), 0)
    low_edge, edge_count = -2 * (span - 1), 4 * span - 1
    bounds = [(2 * chip + low_edge + e) * tokens - 1 for e in range(edge_count)]

    def doc(d, carry):
        start, row, col, counts = carry
        row = row + (start <= places_row).astype(jnp.int32)
        col = col + (start <= places_col).astype(jnp.int32)
        counts = tuple(
            n + jnp.where(start <= bound, 1, 0) for n, bound in zip(counts, bounds)
        )
        return start + docs_ref[d], row, col, counts

    _, seg_row, seg_col, counts = lax.fori_loop(
        0,
        docs_ref.shape[0],
        doc,
        (
            jnp.int32(0),
            jnp.zeros((1, tokens), jnp.int32),
            jnp.zeros((tokens, 1), jnp.int32),
            tuple(jnp.int32(0) for _ in range(edge_count)),
        ),
    )

    def edges(offset):
        return counts[offset - low_edge]

    def keep(offset):
        block = 2 * chip + offset
        inside = (block >= 0) & (block < count)
        return jnp.where(inside, jnp.where(edges(offset) == edges(offset + 1), 1.0, 0.0), 0.0)

    before = jnp.where(core == 0, edges(0), edges(1))
    after = jnp.where(core == 0, edges(1), edges(2))
    rows_ref[0] = jnp.broadcast_to((seg_row == before).astype(f32), (8, tokens))
    rows_ref[1] = jnp.broadcast_to((seg_row == after).astype(f32), (8, tokens))
    for r in range(tokens // 128):
        at = slice(r * 128, (r + 1) * 128)
        jj = r * 128 + lax.broadcasted_iota(jnp.int32, (128, tokens), 0)
        ii = lax.broadcasted_iota(jnp.int32, (128, tokens), 1)
        same = seg_col[at] == seg_row
        mask_ref[at, :] = jnp.where(jj <= ii, jnp.where(same, 1.0, 0.0), 0.0)

    qkt[...] = qk_ref[...].astype(f32).T.astype(bf16)

    def head_rows(h):
        return pl.ds(pl.multiple_of(h * HEAD, HEAD), HEAD)

    def query(h):
        return qkt[pl.ds(pl.multiple_of(h * 2 * QK, QK), QK), :]

    def key(h):
        return qkt[pl.ds(pl.multiple_of(h * 2 * QK + QK, QK), QK), :]

    def feature_factors(points):
        first = mm(lcol_ref[...], points, 1, 0) + cols_ref[:, 0:1]
        second = mm(rcol_ref[...], points, 1, 0) + cols_ref[:, 1:2]
        return first, second

    def feature_grad(grad, first, second):
        scaled = grad * cols_ref[:, 2:3]
        return mm(lrow_ref[...], (scaled * second).astype(bf16), 1, 0) + mm(
            rrow_ref[...], (scaled * first).astype(bf16), 1, 0
        )

    def each_head(first, last, body):
        @pl.loop(first, last)
        def _(h):
            body(h)

    def carry_copies(way, k):
        to = partner if k == 0 else c + 2 * k * (1 - 2 * way)
        src, nsrc = (own, nown) if k == 0 else (pair, npair)
        dst, ndst = (
            (oth.at[way], noth.at[way]) if k == 0 else (arr.at[way, k - 1], narr.at[way, k - 1])
        )
        return [
            pltpu.make_async_remote_copy(
                src_ref=s.at[way],
                dst_ref=d,
                send_sem=c_send.at[way, k, i],
                recv_sem=c_recv.at[way, k, i],
                device_id={"ctx": to, "head": z},
                device_id_type=MESH,
            )
            for i, (s, d) in enumerate(((src, dst), (nsrc, ndst)))
        ]

    def onward(way, k):
        return chip + k < chips if way == 0 else chip >= k

    def behind(way, k):
        return chip >= k if way == 0 else chip + k < chips

    def start_all(copies):
        for copy in copies:
            copy.start()

    def carry_pair(way):
        for copy in carry_copies(way, 0):
            copy.wait_recv()
        keep_near = keep(1 - way)
        early = core == way
        mine = jnp.where(early, keep_near, 1.0)
        theirs = jnp.where(early, 1.0, keep_near)

        def one(h):
            pair[way, h] = (mine * own[way, h].astype(f32) + theirs * oth[way, h].astype(f32)).astype(bf16)
            npair[way, h] = mine * nown[way, h] + theirs * noth[way, h]

        each_head(0, heads, one)
        for k in range(1, span + 1):
            pl.when(onward(way, k))(lambda k=k: start_all(carry_copies(way, k)))

    def carry_arrive(way):
        for k in range(1, span + 1):

            @pl.when(behind(way, k))
            def _(k=k):
                for copy in carry_copies(way, k):
                    copy.wait_recv()

    def carry_total(way, h):
        early = core == way
        near = jnp.where(early, 0.0, 1.0)
        far = jnp.where(early, 1.0, keep(way))
        total, ntotal, through = 0.0, 0.0, far
        for k in range(1, span + 1):
            if k > 1:
                base = 2 * (k - 1) * (2 * way - 1)
                through = through * keep(base) * keep(base + 1)
            there = behind(way, k)
            total = total + through * jnp.where(there, arr[way, k - 1, h].astype(f32), 0.0)
            ntotal = ntotal + through * jnp.where(there, narr[way, k - 1, h], 0.0)
        return near * oth[way, h].astype(f32) + total, near * noth[way, h] + ntotal

    carried_row = rows_ref[0, 0:1]
    ending_row = rows_ref[1, 0:1]
    ones8 = jnp.ones((8, tokens), bf16)

    def features(h):
        first, second = feature_factors(key(h))
        feat = (first * second * cols_ref[:, 2:3] * ending_row).astype(bf16)
        phik[h] = feat
        own[0, h] = (mm(feat, v_ref[:, head_rows(h)], 1, 0) * cols_ref[:, 3:4]).astype(bf16)
        nown[0, h] = mm(ones8, feat, 1, 1) * wrow_ref[...]
        first, second = feature_factors(query(h))
        phiq[h] = (first * second * cols_ref[:, 2:3] * carried_row).astype(bf16)

    each_head(0, heads, features)
    start_all(carry_copies(0, 0))

    blocks = [(slice(0, half_t), half_t), (slice(half_t, tokens), tokens)]

    def scores_of(h, at, upto):
        return mm(key(h)[:, :upto], query(h)[:, at] * bf16(0.25), 0, 0)

    def attend(h):
        for at, upto in blocks:
            s = scores_of(h, at, upto)
            weight = ((0.5 * s + 1.0) * s + 1.0) * mask_ref[:upto, at]
            weight_b = weight.astype(bf16)
            wb_ref[h, :upto, at] = weight_b
            den_ref[h, :, at] = jnp.broadcast_to(
                jnp.sum(weight, axis=0, keepdims=True), (8, half_t)
            )
            y_ref[h, :, at] = mm(v_ref[:upto, head_rows(h)], weight_b, 0, 0)

    third = max(1, heads // 4)
    each_head(0, third, attend)
    carry_pair(0)
    each_head(third, heads // 2, attend)
    if depth > 1:
        arrive(1, 0)
    each_head(heads // 2, heads, attend)
    carry_arrive(0)

    def finish_forward(h):
        state, norm = carry_total(0, h)
        state_b = state.astype(bf16)
        st_ref[h] = state_b
        nin_ref[h] = norm
        feat = phiq[h]
        from_state = mm(state_b, feat, 0, 0)
        from_norm = jnp.sum(mm(split_rows(norm), feat, 1, 0), axis=0, keepdims=True)
        inverse = 1.0 / (den_ref[h, 0:1] + from_norm)
        den_ref[h] = jnp.broadcast_to(inverse, (8, tokens))
        y = (y_ref[h] + from_state) * inverse
        y_ref[h] = y
        att_ref[head_rows(h), :] = y.astype(bf16)

    each_head(0, heads, finish_forward)
    own_copy.wait()

    row_block = min(256, rows_all)
    blocks_of_rows = rows_all // row_block

    def columns(j, which):
        return slice((2 * j + which) * cw, (2 * j + which + 1) * cw)

    def partner_copy(n):
        return pltpu.make_async_remote_copy(
            src_ref=psend.at[n],
            dst_ref=precv.at[n],
            send_sem=p_ssem.at[n],
            recv_sem=p_rsem.at[n],
            device_id={"ctx": partner, "head": z},
            device_id_type=MESH,
        )

    def product(n):
        def halves(mine):
            @pl.loop(0, blocks_of_rows)
            def _(b):
                at = pl.ds(pl.multiple_of(b * row_block, row_block), row_block)
                for j in range(roots):
                    psend[n, at, j * cw : (j + 1) * cw] = mm(
                        att_ref[at, :], out_ref[n, :, columns(j, 1 - mine)], 1, 0
                    ).astype(bf16)

            partner_copy(n).start()

            @pl.loop(0, blocks_of_rows)
            def _(b):
                at = pl.ds(pl.multiple_of(b * row_block, row_block), row_block)
                for j in range(roots):
                    acc[n, at, j * cw : (j + 1) * cw] = mm(
                        att_ref[at, :], out_ref[n, :, columns(j, mine)], 1, 0
                    )

        for mine in range(2):
            pl.when(core == mine)(lambda mine=mine: halves(mine))

    def upstream(n):
        w_copy(n).wait()

        @pl.loop(0, blocks_of_rows)
        def _(b):
            at = pl.ds(pl.multiple_of(b * row_block, row_block), row_block)
            part = mm(wbuf[n % 2, at, :], out_ref[n], 1, 1)
            up_ref[at, :] = part if n == 0 else up_ref[at, :] + part

        if n + 2 < depth:
            w_copy(n + 2).start()

    orders = [list(range(bits))[::-1], list(range(bits))]

    def relative(n, j, b):
        root = piece(n) * roots + j
        return (chip_bit[b] + (root // (1 << b)) % 2) % 2

    def taking_part(n, j, flow, stage):
        live = None
        for b in orders[flow][:stage]:
            here = relative(n, j, b) == 0
            live = here if live is None else live & here
        return live

    def both(a, b):
        return b if a is None else a & b

    def flow_rows(flow):
        return pl.ds(flow * half_r, half_r)

    def flow_columns(j):
        return pl.ds(j * cw, cw)

    def stage_copy(n, j, flow, stage):
        b = orders[flow][stage]
        return pltpu.make_async_remote_copy(
            src_ref=psend.at[n, flow_rows(flow), flow_columns(j)],
            dst_ref=rbuf.at[n, stage, flow_rows(flow), flow_columns(j)],
            send_sem=s_ssem.at[n, flow, j],
            recv_sem=s_rsem.at[n, stage, flow, j],
            device_id={"ctx": neighbour[b], "head": z},
            device_id_type=MESH,
        )

    def result_copy(j, flow):
        return pltpu.make_async_copy(
            pbuf.at[flow_rows(flow), :], p_out.at[flow_rows(flow), :], osem.at[flow]
        )

    def tree(n, step):
        if step == 0:
            partner_copy(n).wait()
        for flow in (0, 1) if step % 2 == 0 else (1, 0):
            for j in range(roots):
                at, cols = flow_rows(flow), slice(j * cw, (j + 1) * cw)
                came = None
                if step == 0:
                    acc[n, at, cols] = acc[n, at, cols] + precv[n, at, cols].astype(f32)
                else:
                    live = taking_part(n, j, flow, step - 1)
                    came = both(live, relative(n, j, orders[flow][step - 1]) == 0)

                    @pl.when(came)
                    def _():
                        stage_copy(n, j, flow, step - 1).wait_recv()
                        total = acc[n, at, cols] + rbuf[n, step - 1, at, cols].astype(f32)
                        if step == bits:
                            pbuf[at, :] = total
                            result_copy(j, flow).start()
                        else:
                            acc[n, at, cols] = total

                if step < bits:
                    live = taking_part(n, j, flow, step)

                    @pl.when(both(live, relative(n, j, orders[flow][step]) == 1))
                    def _():
                        psend[n, at, cols] = acc[n, at, cols].astype(bf16)
                        stage_copy(n, j, flow, step).start()

    for n in range(depth - 1):
        if n > 1:
            arrive(n, 0)
            arrive(n, 1)
        product(n)
        upstream(n)
        tree(n, 0)
        if n == 0:
            arrive(1, 1)
        for k in range(1, bits + 1):
            if n - k >= 0:
                tree(n - k, k)
    last = depth - 1
    if last > 1:
        arrive(last, 0)
        arrive(last, 1)
    product(last)
    upstream(last)

    def start_backward(h):
        up = up_ref[head_rows(h), :]
        inverse = den_ref[h, 0:1]
        den_grad = -jnp.sum(up * y_ref[h], axis=0, keepdims=True) * inverse
        num_grad = (up * inverse).astype(bf16)
        ng_ref[h] = num_grad
        den_rows = jnp.broadcast_to(den_grad, (8, tokens))
        dg_ref[h] = den_rows
        feat = phiq[h]
        own[1, h] = (mm(feat, num_grad, 1, 1) * cols_ref[:, 3:4]).astype(bf16)
        nadj = jnp.sum(mm(split_rows(den_rows), feat, 1, 1), axis=0, keepdims=True)
        nown[1, h] = jnp.broadcast_to(nadj, (8, FEAT)) * wrow_ref[...]

    each_head(0, heads, start_backward)
    start_all(carry_copies(1, 0))
    tree(last, 0)
    for k in range(1, bits + 1):
        if last - k >= 0:
            tree(last - k, k)
    carry_pair(1)

    def key_rows(h):
        return pl.ds(pl.multiple_of(h * 2 * QK + QK, QK), QK)

    def query_rows(h):
        return pl.ds(pl.multiple_of(h * 2 * QK, QK), QK)

    def outer(rows, dense):
        place = lax.broadcasted_iota(jnp.int32, rows.shape, 0)
        high = rows.astype(bf16).astype(f32)
        left = jnp.where(place == 2, rows - high, jnp.where(place < 2, high, 0.0)).astype(bf16)
        place = lax.broadcasted_iota(jnp.int32, dense.shape, 0)
        high = dense.astype(bf16).astype(f32)
        right = jnp.where(place == 1, dense - high, high).astype(bf16)
        return mm(left, right, 0, 0)

    def attention_grad(h):
        value_part = []
        key_part = []
        for at, upto in blocks:
            q4 = query(h)[:, at] * bf16(0.25)
            grad = ng_ref[h, :, at]
            s = mm(key(h)[:, :upto], q4, 0, 0)
            mix = mm(v_ref[:upto, head_rows(h)], grad, 1, 0) + dg_ref[h, 0:1, at]
            score_grad = (mix * (1.0 + s) * mask_ref[:upto, at]).astype(bf16)
            qkg[query_rows(h), at] = mm(key(h)[:, :upto] * bf16(0.25), score_grad, 1, 0)
            key_part.append(mm(score_grad, q4, 1, 1))
            value_part.append(mm(wb_ref[h, :upto, at], grad, 1, 1))
        vg_ref[h, :half_t] = value_part[0] + value_part[1][:half_t]
        vg_ref[h, half_t:] = value_part[1][half_t:]
        key_sum = jnp.concatenate([key_part[0] + key_part[1][:half_t], key_part[1][half_t:]], axis=0)
        qkg[key_rows(h), :] = key_sum.T
        grad = mm(st_ref[h], ng_ref[h], 1, 0) + outer(nin_ref[h], dg_ref[h])
        first, second = feature_factors(query(h))
        qkg[query_rows(h), :] += feature_grad(grad, first, second) * carried_row

    cut = [heads * (r + 1) // (bits + 1) for r in range(bits)]
    low = 0
    for r in range(1, bits + 1):
        each_head(low, cut[r - 1], attention_grad)
        low = cut[r - 1]
        for k in range(r, bits + 1):
            if last + r - k >= 0:
                tree(last + r - k, k)
    each_head(low, heads, attention_grad)

    carry_arrive(1)

    def finish(h):
        adjoint, nadj = carry_total(1, h)
        adjoint_b = adjoint.astype(bf16)
        feat = phik[h]
        v_out[:, head_rows(h)] = (vg_ref[h] + mm(feat, adjoint_b, 0, 0)).astype(bf16)
        grad = mm(adjoint_b, v_ref[:, head_rows(h)], 1, 1) + mm(split_rows(nadj), ones8, 0, 0)
        first, second = feature_factors(key(h))
        qkg[key_rows(h), :] += feature_grad(grad, first, second) * ending_row

    each_head(0, heads, finish)
    qk_out[...] = qkg[...].T.astype(bf16)

    for part in range(2):
        for way in range(2):
            for k in range(depth - 1):
                pl.when(ag_cond(way, k))(
                    lambda way=way, k=k, part=part: ag(way, k, part).wait_send()
                )
    for way in range(2):
        for copy in carry_copies(way, 0):
            copy.wait_send()
        for k in range(1, span + 1):

            @pl.when(onward(way, k))
            def _(way=way, k=k):
                for copy in carry_copies(way, k):
                    copy.wait_send()

    for n in range(depth):
        for j in range(roots):
            for flow in range(2):
                for stage in range(bits):
                    sends = both(
                        taking_part(n, j, flow, stage), relative(n, j, orders[flow][stage]) == 1
                    )
                    pl.when(sends)(
                        lambda n=n, j=j, flow=flow, stage=stage: stage_copy(
                            n, j, flow, stage
                        ).wait_send()
                    )
    for flow in range(2):
        result_copy(0, flow).wait()


def on_device(query_key, values, out_grad, out_weight, doc_lengths):
    tokens = query_key.shape[0]
    rows_all = out_weight.shape[0]
    heads = rows_all // HEAD
    shard = out_grad.shape[1]
    count = lax.axis_size("ctx")
    depth = lax.axis_size("head")
    chips = count // 2
    bits = chips.bit_length() - 1
    roots = chips // depth
    width = out_weight.shape[1] // count
    span = (DOC_MOST // tokens + 1) // 2
    whole = pl.BlockSpec(memory_space=pltpu.VMEM)
    hbm = pl.BlockSpec(memory_space=pl.ANY)
    vmem = pltpu.VMEM
    dma = pltpu.SemaphoreType.DMA
    scratch = [
        vmem((depth, tokens, shard), bf16),
        vmem((2, rows_all, shard), bf16),
        vmem((2 * QK * heads, tokens), bf16),
        vmem((2 * QK * heads, tokens), f32),
        vmem((heads, FEAT, tokens), bf16),
        vmem((heads, FEAT, tokens), bf16),
        vmem((tokens, tokens), f32),
        vmem((heads, tokens, tokens), bf16),
        vmem((heads, HEAD, tokens), f32),
        vmem((rows_all, tokens), bf16),
        vmem((rows_all, tokens), f32),
        vmem((heads, HEAD, tokens), bf16),
        vmem((heads, 8, tokens), f32),
        vmem((heads, 8, tokens), f32),
        vmem((2, 8, tokens), f32),
        vmem((heads, FEAT, HEAD), bf16),
        vmem((heads, 8, FEAT), f32),
        vmem((2, heads, FEAT, HEAD), bf16),
        vmem((2, heads, FEAT, HEAD), bf16),
        vmem((2, heads, FEAT, HEAD), bf16),
        vmem((2, span, heads, FEAT, HEAD), bf16),
        vmem((2, heads, 8, FEAT), f32),
        vmem((2, heads, 8, FEAT), f32),
        vmem((2, heads, 8, FEAT), f32),
        vmem((2, span, heads, 8, FEAT), f32),
        vmem((heads, tokens, HEAD), f32),
        vmem((depth, rows_all, roots * width), f32),
        vmem((depth, rows_all, roots * width), bf16),
        vmem((depth, rows_all, roots * width), bf16),
        vmem((depth, bits, rows_all, roots * width), bf16),
        vmem((rows_all, width), f32),
        dma((2,)),
        dma,
        dma((2,)),
        dma((2, depth, 2)),
        dma((2, depth, 2)),
        dma((2, span + 1, 2)),
        dma((2, span + 1, 2)),
        dma((depth,)),
        dma((depth,)),
        dma((depth, 2, roots)),
        dma((depth, bits, 2, roots)),
    ]
    return pl.pallas_call(
        functools.partial(kernel, count, depth),
        name="step",
        out_shape=(
            jax.ShapeDtypeStruct(query_key.shape, bf16),
            jax.ShapeDtypeStruct(values.shape, bf16),
            jax.ShapeDtypeStruct((rows_all, width), f32),
        ),
        in_specs=[
            pl.BlockSpec(memory_space=pltpu.SMEM),
            whole,
            whole,
            hbm,
            hbm,
            whole,
            whole,
            whole,
            whole,
            whole,
            whole,
        ],
        out_specs=(whole, whole, hbm),
        scratch_shapes=scratch,
        compiler_params=pltpu.CompilerParams(
            collective_id=0, has_side_effects=True, vmem_limit_bytes=67_043_328
        ),
    )(
        doc_lengths,
        query_key,
        values,
        out_grad,
        out_weight,
        jnp.asarray(LEFT, bf16),
        jnp.asarray(RIGHT, bf16),
        jnp.asarray(LEFT.T, bf16),
        jnp.asarray(RIGHT.T, bf16),
        jnp.asarray(COLS),
        jnp.asarray(np.broadcast_to(COLS[:, 3][None], (8, FEAT)).copy()),
    )


def solution(mesh):
    placed = (P("ctx", "head"), P("ctx", "head"), P("ctx", "head"), P("head", None), P())
    return jax.shard_map(
        on_device,
        mesh=mesh,
        in_specs=placed,
        out_specs=(P("ctx", "head"), P("ctx", "head"), P("head", "ctx")),
        check_vma=False,
    )
```

profile of v0, /device:TPU:26, one launch (start us, length us, event | category | flops | bytes accessed | tf_op | source)
XLA Modules:
  0.0 131.7 jit_solution(15703074341439533745)
XLA Ops:
  0.6 125.6 %step.1 = (bf16[512,256]{1,0:T(8,128)(2,1)}, bf16[512,1024]{1,0:T(8,128)(2,1)}, f32[1024,512]{1,0:T(8,128)}) custom-call(s32[32]{0:T(128)} %docs_ref.1, bf16[512,256]{1,0:T(8,128)(2,1)} %qk_ref.1, bf16[512,1024]{1,0:T(8,128)(2,1)} %v_ref.1, bf16[512,1024]{1,0:T(8,128)(2,1)} %g_ref.1, bf16[1024,4096]{1,0:T(8,128)(2,1)} %w_ref.1, ...), custom_call_target="tpu_custom_call" | custom-call | tf_op jit(solution)/shard_map/step/pallas_call | solution.py:749
  126.3 0.0 copy-start
  126.3 1.8 %copy.17 = bf16[512,256]{1,0:T(8,128)(2,1)} copy(bf16[512,256]{1,0:T(8,128)(2,1)} %get-tuple-element.6) | data formatting | bytes 524288
  128.1 2.3 %copy.18 = bf16[512,1024]{1,0:T(8,128)(2,1)} copy(bf16[512,1024]{1,0:T(8,128)(2,1)} %get-tuple-element.7) | data formatting | bytes 2097152
  130.4 0.0 copy-done
  130.4 1.3 %copy.19 = f32[1024,512]{1,0:T(8,128)} copy(f32[1024,512]{1,0:T(8,128)S(1)} %copy-done) | data formatting | bytes 4194304
Async XLA Ops:
  126.3 4.1 %copy-start = (f32[1024,512]{1,0:T(8,128)S(1)}, f32[1024,512]{1,0:T(8,128)}, u32[]{:S(2)}) copy-start(f32[1024,512]{1,0:T(8,128)} %get-tuple-element.8) | copy-start | bytes 6291460
where the time goes:
time: 132 us
  Pallas kernels  126 us (95%)
  local copies, waits for them, and re-layouts  5.4 us (4%)
    pallas_call x1, Pallas kernels, on_device(): pl.pallas_call(functools.partial(kernel, count, depth), name='step', out_...  126 us
    unnamed x5, local copies, waits for them, and re-layouts  5.4 us

commit v1 on v0

v1 whole, which is shorter than its diff:
```python
import functools
import math

import jax
import jax.numpy as jnp
import numpy as np
from jax import lax
from jax.experimental import pallas as pl
from jax.experimental.pallas import tpu as pltpu
from jax.sharding import PartitionSpec as P

HEAD = 128
QK = 16
DOC_MOST = 2048
LAG = 2

quad_scale = 0.25 / math.sqrt(2.0)

bf16 = jnp.bfloat16
f32 = jnp.float32
MESH = pl.DeviceIdType.MESH

PAIRS = [(a, b) for a in range(QK) for b in range(a, QK)]
FEAT = 160


def tables():
    left = np.zeros((FEAT, QK), np.float32)
    right = np.zeros((FEAT, QK), np.float32)
    cols = np.zeros((FEAT, 4), np.float32)
    cols[0, 0] = cols[0, 1] = cols[0, 2] = 1.0
    cols[:, 3] = 1.0
    for a in range(QK):
        left[1 + a, a] = 1.0
        cols[1 + a, 1] = 1.0
        cols[1 + a, 2] = 0.5
    for place, (a, b) in enumerate(PAIRS):
        left[1 + QK + place, a] = 1.0
        right[1 + QK + place, b] = 1.0
        cols[1 + QK + place, 2] = quad_scale
        cols[1 + QK + place, 3] = 1.0 if a == b else 2.0
    return left, right, cols


LEFT, RIGHT, COLS = tables()


def mm(a, b, ca, cb):
    return lax.dot_general(a, b, (((ca,), (cb,)), ((), ())), preferred_element_type=f32)


def split_rows(rows):
    high = rows.astype(bf16).astype(f32)
    place = lax.broadcasted_iota(jnp.int32, rows.shape, 0)
    return jnp.where(place == 0, high, jnp.where(place == 1, rows - high, 0.0)).astype(bf16)


def kernel(
    count,
    depth,
    docs_ref,
    qk_hbm,
    v_hbm,
    g_ref,
    w_ref,
    lcol_ref,
    rcol_ref,
    lrow_ref,
    rrow_ref,
    cols_ref,
    wrow_ref,
    qk_out,
    v_out,
    p_out,
    qk_ref,
    v_ref,
    v_held,
    out_ref,
    wbuf,
    qkt,
    qkg,
    phiq,
    phik,
    mask_ref,
    slope_ref,
    wb_ref,
    y_ref,
    att_ref,
    up_ref,
    ng_ref,
    den_ref,
    dg_ref,
    rows_ref,
    st_ref,
    own,
    oth,
    pair,
    arr,
    tot,
    nown,
    noth,
    npair,
    narr,
    ntot,
    vg_ref,
    acc,
    psend,
    precv,
    rbuf,
    pbuf,
    isem,
    wsem,
    gsem,
    osem,
    ag_send,
    ag_recv,
    c_send,
    c_recv,
    p_ssem,
    p_rsem,
    s_ssem,
    s_rsem,
):
    tokens = qk_hbm.shape[0]
    heads = v_hbm.shape[1] // HEAD
    rows_all = heads * HEAD
    shard = g_ref.shape[1]
    chips = count // 2
    bits = chips.bit_length() - 1
    roots = chips // depth
    cw = shard // (2 * roots)
    half_t = tokens // 2
    half_h = heads // 2
    shares = acc.shape[0] // depth
    cg = cw // shares
    half_r = rows_all // 2
    span = arr.shape[1]
    c = lax.axis_index("ctx")
    z = lax.axis_index("head")
    chip = c // 2
    core = c % 2
    other_core = 1 - core
    partner = 2 * chip + other_core
    chip_bit = [(chip // (1 << b)) % 2 for b in range(bits)]
    neighbour = [2 * (chip + (1 - 2 * chip_bit[b]) * (1 << b)) + core for b in range(bits)]

    barrier = pltpu.get_barrier_semaphore()

    met = [(None, {"ctx": partner, "head": z})]
    met += [(z > 0, {"ctx": c, "head": z - 1}), (z < depth - 1, {"ctx": c, "head": z + 1})]
    met += [(None, {"ctx": neighbour[b], "head": z}) for b in range(bits) if (1 << b) > span]
    for k in range(1, span + 1):
        met += [
            (chip >= k, {"ctx": c - 2 * k, "head": z}),
            (chip + k < chips, {"ctx": c + 2 * k, "head": z}),
        ]
    peers = 0
    for cond, where in met:

        def greet(where=where):
            pl.semaphore_signal(barrier, inc=1, device_id=where, device_id_type=MESH)

        if cond is None:
            greet()
            peers = peers + 1
        else:
            pl.when(cond)(greet)
            peers = peers + cond.astype(jnp.int32)
    pl.semaphore_wait(barrier, peers)

    def piece(n):
        if n == 0:
            return z
        k = (n + 1) // 2
        inner = z - k if n % 2 else z + k
        low_side = 1 - (2 * z + 1) // depth
        lesser = low_side * z + (1 - low_side) * (depth - 1 - z)
        outer = low_side * n + (1 - low_side) * (depth - 1 - n)
        beyond = (n - 2 * lesser - 1 + 4 * depth) // (4 * depth)
        return (1 - beyond) * inner + beyond * outer

    def slot(way, k, level):
        if k == 0:
            return 0
        low_side = 1 - (2 * level + 1) // depth
        lesser = low_side * level + (1 - low_side) * (depth - 1 - level)
        beyond = (k - lesser - 1 + 2 * depth) // (2 * depth)
        return (1 - beyond) * (2 * k - 1 + way) + beyond * (lesser + k)

    parts = [(g, j, which) for g in range(shares) for j in range(roots) for which in range(2)]

    def part_slice(part):
        g, j, which = parts[part]
        return pl.ds((2 * j + which) * cw + g * cg, cg)

    def held_at(place, part):
        g, j, which = parts[part]
        return out_ref.at[place, g, :, pl.ds((2 * j + which) * cg, cg)]

    def ag(way, k, part):
        to = z + 1 - 2 * way
        if k == 0:
            src = g_ref.at[:, part_slice(part)]
        else:
            src = held_at(slot(way, k, z), part)
        return pltpu.make_async_remote_copy(
            src_ref=src,
            dst_ref=held_at(slot(way, k + 1, to), part),
            send_sem=ag_send.at[way, k, part],
            recv_sem=ag_recv.at[way, k, part],
            device_id={"ctx": c, "head": to},
            device_id_type=MESH,
        )

    def ag_arrival(way, k, part):
        came = held_at(slot(way, k, z), part)
        return pltpu.make_async_remote_copy(
            src_ref=came,
            dst_ref=came,
            send_sem=ag_send.at[way, k, part],
            recv_sem=ag_recv.at[way, k - 1, part],
            device_id={"ctx": c, "head": z - 1 + 2 * way},
            device_id_type=MESH,
        )

    def ag_cond(way, k):
        if way == 0:
            return (z >= k) & (z < depth - 1)
        return (z + k <= depth - 1) & (z > 0)

    def ag_has(way, k):
        return z >= k if way == 0 else z + k <= depth - 1

    for part in range(len(parts)):
        for way in range(2):
            pl.when(ag_cond(way, 0))(lambda way=way, part=part: ag(way, 0, part).start())

    def arrive(k, share):
        for part in range(len(parts)):
            for way in range(2):
                if parts[part][0] == share:

                    @pl.when(ag_has(way, k))
                    def _(way=way, part=part):
                        ag_arrival(way, k, part).wait_recv()

                    if k < depth - 1:
                        pl.when(ag_cond(way, k))(
                            lambda way=way, part=part: ag(way, k, part).start()
                        )

    own_copies = [
        pltpu.make_async_copy(g_ref.at[:, part_slice(part)], held_at(0, part), gsem.at[part])
        for part in range(len(parts))
    ]
    for copy in own_copies:
        copy.start()

    def w_copies(n):
        at = piece(n) * shard
        copies = []
        for part, (g, j, which) in enumerate(parts):
            start = pl.multiple_of(at + ((2 * j + which) * cw + g * cg), cg)
            copies.append(
                pltpu.make_async_copy(
                    w_ref.at[:, pl.ds(start, cg)],
                    wbuf.at[n % 2, g, :, pl.ds((2 * j + which) * cg, cg)],
                    wsem.at[n % 2, part],
                )
            )
        return copies

    def start_all(copies):
        for copy in copies:
            copy.start()

    for n in range(min(2, depth)):
        start_all(w_copies(n))

    inputs = [
        pltpu.make_async_copy(qk_hbm, qk_ref, isem.at[0]),
        pltpu.make_async_copy(v_hbm, v_ref, isem.at[1]),
    ]
    start_all(inputs)

    places_row = c * tokens + lax.broadcasted_iota(jnp.int32, (1, tokens), 1)
    places_col = c * tokens + lax.broadcasted_iota(jnp.int32, (tokens, 1), 0)
    low_edge, edge_count = -2 * (span - 1), 4 * span - 1
    bounds = [(2 * chip + low_edge + e) * tokens - 1 for e in range(edge_count)]

    def doc(d, carry):
        start, row, col, counts = carry
        row = row + (start <= places_row).astype(jnp.int32)
        col = col + (start <= places_col).astype(jnp.int32)
        counts = tuple(
            n + jnp.where(start <= bound, 1, 0) for n, bound in zip(counts, bounds)
        )
        return start + docs_ref[d], row, col, counts

    _, seg_row, seg_col, counts = lax.fori_loop(
        0,
        docs_ref.shape[0],
        doc,
        (
            jnp.int32(0),
            jnp.zeros((1, tokens), jnp.int32),
            jnp.zeros((tokens, 1), jnp.int32),
            tuple(jnp.int32(0) for _ in range(edge_count)),
        ),
    )

    def edges(offset):
        return counts[offset - low_edge]

    def keep(offset):
        block = 2 * chip + offset
        inside = (block >= 0) & (block < count)
        return jnp.where(inside, jnp.where(edges(offset) == edges(offset + 1), 1.0, 0.0), 0.0)

    before = jnp.where(core == 0, edges(0), edges(1))
    after = jnp.where(core == 0, edges(1), edges(2))
    rows_ref[0] = jnp.broadcast_to((seg_row == before).astype(f32), (8, tokens))
    rows_ref[1] = jnp.broadcast_to((seg_row == after).astype(f32), (8, tokens))
    for r in range(tokens // 128):
        at = slice(r * 128, (r + 1) * 128)
        jj = r * 128 + lax.broadcasted_iota(jnp.int32, (128, tokens), 0)
        ii = lax.broadcasted_iota(jnp.int32, (128, tokens), 1)
        same = seg_col[at] == seg_row
        mask_ref[at, :] = jnp.where(jj <= ii, jnp.where(same, 1.0, 0.0), 0.0)

    for copy in inputs:
        copy.wait()
    qkt[...] = qk_ref[...].astype(f32).T.astype(bf16)

    def head_rows(h):
        return pl.ds(pl.multiple_of(h * HEAD, HEAD), HEAD)

    def query(h):
        return qkt[pl.ds(pl.multiple_of(h * 2 * QK, QK), QK), :]

    def key(h):
        return qkt[pl.ds(pl.multiple_of(h * 2 * QK + QK, QK), QK), :]

    def feature_factors(points):
        first = mm(lcol_ref[...], points, 1, 0) + cols_ref[:, 0:1]
        second = mm(rcol_ref[...], points, 1, 0) + cols_ref[:, 1:2]
        return first, second

    def feature_grad(grad, first, second):
        scaled = grad * cols_ref[:, 2:3]
        return mm(lrow_ref[...], (scaled * second).astype(bf16), 1, 0) + mm(
            rrow_ref[...], (scaled * first).astype(bf16), 1, 0
        )

    def each_head(first, last, body):
        @pl.loop(first, last)
        def _(h):
            body(h)

    def my_heads():
        return pl.ds(core * half_h, half_h)

    def carry_copies(way, k):
        to = c + 2 * k * (1 - 2 * way) if k > 0 else partner
        if k == 0:
            moves = [(own.at[way], oth.at[way]), (nown.at[way], noth.at[way])]
        elif k > 0:
            moves = [(pair.at[way], arr.at[way, k - 1]), (npair.at[way], narr.at[way, k - 1])]
        else:
            moves = [(tot.at[way, my_heads()], tot.at[way, my_heads()])]
        at = k if k >= 0 else span + 1
        return [
            pltpu.make_async_remote_copy(
                src_ref=src,
                dst_ref=dst,
                send_sem=c_send.at[way, at, i],
                recv_sem=c_recv.at[way, at, i],
                device_id={"ctx": to, "head": z},
                device_id_type=MESH,
            )
            for i, (src, dst) in enumerate(moves)
        ]

    def total_arrival(way):
        came = tot.at[way, pl.ds(other_core * half_h, half_h)]
        return pltpu.make_async_remote_copy(
            src_ref=came,
            dst_ref=came,
            send_sem=c_send.at[way, span + 1, 0],
            recv_sem=c_recv.at[way, span + 1, 0],
            device_id={"ctx": partner, "head": z},
            device_id_type=MESH,
        )

    def onward(way, k):
        return chip + k < chips if way == 0 else chip >= k

    def behind(way, k):
        return chip >= k if way == 0 else chip + k < chips

    def carry_pair(way):
        for copy in carry_copies(way, 0):
            copy.wait_recv()
        keep_near = keep(1 - way)
        early = core == way
        mine = jnp.where(early, keep_near, 1.0)
        theirs = jnp.where(early, 1.0, keep_near)

        @pl.loop(0, half_h)
        def _(i):
            h = core * half_h + i
            pair[way, i] = (mine * own[way, h].astype(f32) + theirs * oth[way, h].astype(f32)).astype(bf16)

        npair[way] = mine * nown[way] + theirs * noth[way]
        for k in range(1, span + 1):
            pl.when(onward(way, k))(lambda k=k: start_all(carry_copies(way, k)))

    def carry_arrive(way):
        for k in range(1, span + 1):

            @pl.when(behind(way, k))
            def _(k=k):
                for copy in carry_copies(way, k):
                    copy.wait_recv()

        through = [jnp.float32(1.0)]
        for k in range(2, span + 1):
            base = 2 * (k - 1) * (2 * way - 1)
            through.append(through[-1] * keep(base) * keep(base + 1))

        def weighed(stack, index):
            total = 0.0
            for k in range(1, span + 1):
                came = jnp.where(behind(way, k), stack[(way, k - 1) + index].astype(f32), 0.0)
                total = total + through[k - 1] * came
            return total

        @pl.loop(0, half_h)
        def _(i):
            tot[way, core * half_h + i] = weighed(arr, (i,)).astype(bf16)

        start_all(carry_copies(way, -1))
        near, far = carry_shares(way)
        ntot[way] = near * noth[way] + far * weighed(narr, ())

    def carry_shares(way):
        early = core == way
        return jnp.where(early, 0.0, 1.0), jnp.where(early, 1.0, keep(way))

    def carry_total(way, h):
        near, far = carry_shares(way)
        norm = jnp.broadcast_to(ntot[way, pl.ds(h, 1), :], (8, FEAT))
        return near * oth[way, h].astype(f32) + far * tot[way, h].astype(f32), norm

    carried_row = rows_ref[0, 0:1]
    ending_row = rows_ref[1, 0:1]
    ones8 = jnp.ones((8, tokens), bf16)

    def features(h):
        first, second = feature_factors(key(h))
        feat = (first * second * cols_ref[:, 2:3] * ending_row).astype(bf16)
        phik[h] = feat
        own[0, h] = (mm(feat, v_ref[:, head_rows(h)], 1, 0) * cols_ref[:, 3:4]).astype(bf16)
        nown[0, pl.ds(h, 1), :] = (mm(ones8, feat, 1, 1) * wrow_ref[...])[0:1]
        first, second = feature_factors(query(h))
        phiq[h] = (first * second * cols_ref[:, 2:3] * carried_row).astype(bf16)

    each_head(0, heads, features)
    start_all(carry_copies(0, 0))

    blocks = [(slice(0, half_t), half_t), (slice(half_t, tokens), tokens)]

    def scores_of(h, at, upto):
        return mm(key(h)[:, :upto], query(h)[:, at] * bf16(0.25), 0, 0)

    def attend(h):
        for at, upto in blocks:
            s = scores_of(h, at, upto)
            slope_ref[h, :upto, at] = (1.0 + s) * mask_ref[:upto, at]
            weight = ((0.5 * s + 1.0) * s + 1.0) * mask_ref[:upto, at]
            weight_b = weight.astype(bf16)
            wb_ref[h, :upto, at] = weight_b
            den_ref[h, :, at] = jnp.broadcast_to(
                jnp.sum(weight, axis=0, keepdims=True), (8, half_t)
            )
            y_ref[h, :, at] = mm(v_ref[:upto, head_rows(h)], weight_b, 0, 0)

    each_head(0, heads // 4, attend)
    carry_pair(0)
    each_head(heads // 4, heads // 2, attend)
    arrive(1, 0)
    each_head(heads // 2, 3 * heads // 4, attend)
    carry_arrive(0)
    each_head(3 * heads // 4, heads, attend)
    total_arrival(0).wait_recv()

    def finish_forward(h):
        state, norm = carry_total(0, h)
        state_b = state.astype(bf16)
        st_ref[h] = state_b
        feat = phiq[h]
        from_state = mm(state_b, feat, 0, 0)
        from_norm = jnp.sum(mm(split_rows(norm), feat, 1, 0), axis=0, keepdims=True)
        inverse = 1.0 / (den_ref[h, 0:1] + from_norm)
        den_ref[h] = jnp.broadcast_to(inverse, (8, tokens))
        y = (y_ref[h] + from_state) * inverse
        y_ref[h] = y
        att_ref[head_rows(h), :] = y.astype(bf16)

    each_head(0, heads, finish_forward)
    for copy in own_copies:
        copy.wait()

    row_block = min(256, rows_all)
    blocks_of_rows = rows_all // row_block

    def partner_copy(m):
        return pltpu.make_async_remote_copy(
            src_ref=psend.at[m],
            dst_ref=precv.at[m],
            send_sem=p_ssem.at[m],
            recv_sem=p_rsem.at[m],
            device_id={"ctx": partner, "head": z},
            device_id_type=MESH,
        )

    def product(m):
        n, g = m // shares, m % shares

        @pl.loop(0, blocks_of_rows)
        def _(b):
            at = pl.ds(pl.multiple_of(b * row_block, row_block), row_block)
            both_cores = mm(att_ref[at, :], out_ref[n, g], 1, 0)
            for mine in range(2):

                @pl.when(core == mine)
                def _():
                    for j in range(roots):
                        to = slice(j * cg, (j + 1) * cg)
                        theirs = (2 * j + 1 - mine) * cg
                        ours = (2 * j + mine) * cg
                        psend[m, at, to] = both_cores[:, theirs : theirs + cg].astype(bf16)
                        acc[m, at, to] = both_cores[:, ours : ours + cg]

        partner_copy(m).start()

    def upstream(m):
        n, g = m // shares, m % shares
        if g == 0:
            for copy in w_copies(n):
                copy.wait()

        @pl.loop(0, blocks_of_rows)
        def _(b):
            at = pl.ds(pl.multiple_of(b * row_block, row_block), row_block)
            one = mm(wbuf[n % 2, g, at, :], out_ref[n, g], 1, 1)
            up_ref[at, :] = one if m == 0 else up_ref[at, :] + one

        if g == shares - 1 and n + 2 < depth:
            start_all(w_copies(n + 2))

    if bits == 2:
        flows = [
            [({one: 1, two: 0}, two), ({one: 1, two: 1}, one), ({one: 0, two: 1}, two)]
            for one, two in ((0, 1), (1, 0))
        ]
    else:
        flows = []
        for order in (list(range(bits))[::-1], list(range(bits))):
            done = [dict.fromkeys(order[:stage], 0) for stage in range(bits)]
            flows.append([({**done[stage], b: 1}, b) for stage, b in enumerate(order)])
    stages = len(flows[0])

    def relative(m, j, b):
        root = piece(m // shares) * roots + j
        return (chip_bit[b] + (root // (1 << b)) % 2) % 2

    def matches(m, j, pattern):
        live = None
        for b, value in pattern.items():
            here = relative(m, j, b) == value
            live = here if live is None else live & here
        return live

    def sends(m, j, flow, stage):
        return matches(m, j, flows[flow][stage][0])

    def receives(m, j, flow, stage):
        pattern, b = flows[flow][stage]
        return matches(m, j, {**pattern, b: 1 - pattern[b]})

    def inbox(stage):
        return stage % rbuf.shape[1]

    def flow_rows(flow):
        return pl.ds(flow * half_r, half_r)

    def flow_columns(j):
        return pl.ds(j * cg, cg)

    def stage_copy(m, j, flow, stage):
        b = flows[flow][stage][1]
        return pltpu.make_async_remote_copy(
            src_ref=psend.at[m, flow_rows(flow), flow_columns(j)],
            dst_ref=rbuf.at[m, inbox(stage), flow_rows(flow), flow_columns(j)],
            send_sem=s_ssem.at[m, flow, j],
            recv_sem=s_rsem.at[m, inbox(stage), flow, j],
            device_id={"ctx": neighbour[b], "head": z},
            device_id_type=MESH,
        )

    def result_copy(g, flow):
        return pltpu.make_async_copy(
            pbuf.at[g, flow_rows(flow), :],
            p_out.at[flow_rows(flow), pl.ds(g * cg, cg)],
            osem.at[g, flow],
        )

    def tree(m, step):
        if step == 0:
            partner_copy(m).wait()
        for flow in range(2):
            for j in range(roots):
                at, cols = flow_rows(flow), slice(j * cg, (j + 1) * cg)
                if step == 0:
                    acc[m, at, cols] = acc[m, at, cols] + precv[m, at, cols].astype(f32)
                else:

                    @pl.when(receives(m, j, flow, step - 1))
                    def _():
                        stage_copy(m, j, flow, step - 1).wait_recv()
                        total = acc[m, at, cols] + rbuf[m, inbox(step - 1), at, cols].astype(f32)
                        if step == stages:
                            pbuf[m % shares, at, :] = total
                            result_copy(m % shares, flow).start()
                        else:
                            acc[m, at, cols] = total

                if step < stages:

                    @pl.when(sends(m, j, flow, step))
                    def _():
                        psend[m, at, cols] = acc[m, at, cols].astype(bf16)
                        stage_copy(m, j, flow, step).start()

    last = depth * shares - 1

    def trees(m):
        for step in range(stages + 1):
            if 0 <= m - LAG * step <= last:
                tree(m - LAG * step, step)

    for m in range(last):
        if m >= 2 * shares:
            arrive(m // shares, m % shares)
        if 0 < m < shares:
            arrive(1, m)
        product(m)
        upstream(m)
        trees(m)
    arrive(last // shares, last % shares)
    product(last)
    upstream(last)

    def start_backward(h):
        up = up_ref[head_rows(h), :]
        inverse = den_ref[h, 0:1]
        den_grad = -jnp.sum(up * y_ref[h], axis=0, keepdims=True) * inverse
        num_grad = (up * inverse).astype(bf16)
        ng_ref[h] = num_grad
        den_rows = jnp.broadcast_to(den_grad, (8, tokens))
        dg_ref[h] = den_rows
        feat = phiq[h]
        own[1, h] = (mm(feat, num_grad, 1, 1) * cols_ref[:, 3:4]).astype(bf16)
        nadj = jnp.sum(mm(split_rows(den_rows), feat, 1, 1), axis=0, keepdims=True)
        nown[1, pl.ds(h, 1), :] = nadj * wrow_ref[0:1]

    each_head(0, heads, start_backward)
    start_all(carry_copies(1, 0))
    trees(last)
    carry_pair(1)

    def key_rows(h):
        return pl.ds(pl.multiple_of(h * 2 * QK + QK, QK), QK)

    def query_rows(h):
        return pl.ds(pl.multiple_of(h * 2 * QK, QK), QK)

    def outer(rows, dense):
        place = lax.broadcasted_iota(jnp.int32, rows.shape, 0)
        high = rows.astype(bf16).astype(f32)
        left = jnp.where(place == 2, rows - high, jnp.where(place < 2, high, 0.0)).astype(bf16)
        place = lax.broadcasted_iota(jnp.int32, dense.shape, 0)
        high = dense.astype(bf16).astype(f32)
        right = jnp.where(place == 1, dense - high, high).astype(bf16)
        return mm(left, right, 0, 0)

    def attention_grad(h):
        value_part = []
        key_part = []
        for at, upto in blocks:
            q4 = query(h)[:, at] * bf16(0.25)
            grad = ng_ref[h, :, at]
            mix = mm(v_ref[:upto, head_rows(h)], grad, 1, 0) + dg_ref[h, 0:1, at]
            score_grad = (mix * slope_ref[h, :upto, at]).astype(bf16)
            qkg[query_rows(h), at] = mm(key(h)[:, :upto] * bf16(0.25), score_grad, 1, 0)
            key_part.append(mm(score_grad, q4, 1, 1))
            value_part.append(mm(wb_ref[h, :upto, at], grad, 1, 1))
        vg_ref[h, :half_t] = value_part[0] + value_part[1][:half_t]
        vg_ref[h, half_t:] = value_part[1][half_t:]
        key_sum = jnp.concatenate([key_part[0] + key_part[1][:half_t], key_part[1][half_t:]], axis=0)
        qkg[key_rows(h), :] = key_sum.T
        grad = mm(st_ref[h], ng_ref[h], 1, 0) + outer(jnp.broadcast_to(ntot[0, pl.ds(h, 1), :], (8, FEAT)), dg_ref[h])
        first, second = feature_factors(query(h))
        qkg[query_rows(h), :] += feature_grad(grad, first, second) * carried_row

    rounds = LAG * stages
    steps = 2 * heads

    def remaining(at):
        for r in range(at * rounds // steps, (at + 1) * rounds // steps):
            trees(last + 1 + r)

    for h in range(heads):
        each_head(h, h + 1, attention_grad)
        remaining(h)
        if h == heads // 2:
            carry_arrive(1)

    total_arrival(1).wait_recv()

    def finish(h):
        adjoint, nadj = carry_total(1, h)
        adjoint_b = adjoint.astype(bf16)
        feat = phik[h]
        v_held[:, head_rows(h)] = (vg_ref[h] + mm(feat, adjoint_b, 0, 0)).astype(bf16)
        grad = mm(adjoint_b, v_ref[:, head_rows(h)], 1, 1) + mm(split_rows(nadj), ones8, 0, 0)
        first, second = feature_factors(key(h))
        qkg[key_rows(h), :] += feature_grad(grad, first, second) * ending_row

    for h in range(heads):
        each_head(h, h + 1, finish)
        remaining(heads + h)
    qk_ref[...] = qkg[...].T.astype(bf16)
    outputs = [
        pltpu.make_async_copy(qk_ref, qk_out, isem.at[0]),
        pltpu.make_async_copy(v_held, v_out, isem.at[1]),
    ]
    start_all(outputs)

    for part in range(len(parts)):
        for way in range(2):
            for k in range(depth - 1):
                pl.when(ag_cond(way, k))(
                    lambda way=way, k=k, part=part: ag(way, k, part).wait_send()
                )
    for way in range(2):
        for copy in carry_copies(way, 0) + carry_copies(way, -1):
            copy.wait_send()
        for k in range(1, span + 1):

            @pl.when(onward(way, k))
            def _(way=way, k=k):
                for copy in carry_copies(way, k):
                    copy.wait_send()

    for m in range(last + 1):
        for j in range(roots):
            for flow in range(2):
                for stage in range(stages):
                    pl.when(sends(m, j, flow, stage))(
                        lambda m=m, j=j, flow=flow, stage=stage: stage_copy(
                            m, j, flow, stage
                        ).wait_send()
                    )
    for g in range(shares):
        for flow in range(2):
            result_copy(g, flow).wait()
    for copy in outputs:
        copy.wait()


def hand_on_kernel(cuts, *refs):
    count = len(cuts)
    sources, targets, held = refs[:count], refs[count : 2 * count], refs[2 * count : 3 * count]
    sem_in, sem_out = refs[3 * count :]
    moves = []
    for n, cut in enumerate(cuts):
        size = sources[n].shape[0] // cut
        for at in range(cut):
            rows = pl.ds(at * size, size)
            place = len(moves)
            moves.append(
                (
                    pltpu.make_async_copy(sources[n].at[rows], held[n].at[rows], sem_in.at[place]),
                    pltpu.make_async_copy(held[n].at[rows], targets[n].at[rows], sem_out.at[place]),
                )
            )
    for come, _ in moves:
        come.start()
    for come, go in moves:
        come.wait()
        go.start()
    for _, go in moves:
        go.wait()


def hand_on(*arrays):
    cuts = [max(1, a.size * a.dtype.itemsize >> 18) for a in arrays]
    hbm = pl.BlockSpec(memory_space=pl.ANY)
    return pl.pallas_call(
        functools.partial(hand_on_kernel, cuts),
        name="hand_on",
        out_shape=tuple(jax.ShapeDtypeStruct(a.shape, a.dtype) for a in arrays),
        in_specs=[hbm] * len(arrays),
        out_specs=(hbm,) * len(arrays),
        scratch_shapes=[pltpu.VMEM(a.shape, a.dtype) for a in arrays]
        + [pltpu.SemaphoreType.DMA((sum(cuts),)), pltpu.SemaphoreType.DMA((sum(cuts),))],
    )(*arrays)


def on_device(query_key, values, out_grad, out_weight, doc_lengths):
    tokens = query_key.shape[0]
    rows_all = out_weight.shape[0]
    heads = rows_all // HEAD
    count = lax.axis_size("ctx")
    depth = lax.axis_size("head")
    chips = count // 2
    bits = chips.bit_length() - 1
    roots = chips // depth
    width = out_weight.shape[1] // count
    span = (DOC_MOST // tokens + 1) // 2
    shares = max(1, min(4, width // 128))
    inboxes = 1 if bits == 2 else bits
    wide = roots * width // shares
    parts = 2 * roots * shares
    pieces = depth * shares
    whole = pl.BlockSpec(memory_space=pltpu.VMEM)
    hbm = pl.BlockSpec(memory_space=pl.ANY)
    vmem = pltpu.VMEM
    dma = pltpu.SemaphoreType.DMA
    scratch = [
        vmem(query_key.shape, bf16),
        vmem(values.shape, bf16),
        vmem(values.shape, bf16),
        vmem((depth, shares, tokens, 2 * wide), bf16),
        vmem((2, shares, rows_all, 2 * wide), bf16),
        vmem((2 * QK * heads, tokens), bf16),
        vmem((2 * QK * heads, tokens), f32),
        vmem((heads, FEAT, tokens), bf16),
        vmem((heads, FEAT, tokens), bf16),
        vmem((tokens, tokens), f32),
        vmem((heads, tokens, tokens), f32),
        vmem((heads, tokens, tokens), bf16),
        vmem((heads, HEAD, tokens), f32),
        vmem((rows_all, tokens), bf16),
        vmem((rows_all, tokens), f32),
        vmem((heads, HEAD, tokens), bf16),
        vmem((heads, 8, tokens), f32),
        vmem((heads, 8, tokens), f32),
        vmem((2, 8, tokens), f32),
        vmem((heads, FEAT, HEAD), bf16),
        vmem((2, heads, FEAT, HEAD), bf16),
        vmem((2, heads, FEAT, HEAD), bf16),
        vmem((2, heads // 2, FEAT, HEAD), bf16),
        vmem((2, span, heads // 2, FEAT, HEAD), bf16),
        vmem((2, heads, FEAT, HEAD), bf16),
        vmem((2, heads, FEAT), f32),
        vmem((2, heads, FEAT), f32),
        vmem((2, heads, FEAT), f32),
        vmem((2, span, heads, FEAT), f32),
        vmem((2, heads, FEAT), f32),
        vmem((heads, tokens, HEAD), f32),
        vmem((pieces, rows_all, wide), f32),
        vmem((pieces, rows_all, wide), bf16),
        vmem((pieces, rows_all, wide), bf16),
        vmem((pieces, inboxes, rows_all, wide), bf16),
        vmem((shares, rows_all, width // shares), f32),
        dma((2,)),
        dma((2, parts)),
        dma((parts,)),
        dma((shares, 2)),
        dma((2, depth, parts)),
        dma((2, depth, parts)),
        dma((2, span + 2, 2)),
        dma((2, span + 2, 2)),
        dma((pieces,)),
        dma((pieces,)),
        dma((pieces, 2, roots)),
        dma((pieces, inboxes, 2, roots)),
    ]
    results = pl.pallas_call(
        functools.partial(kernel, count, depth),
        name="step",
        out_shape=(
            jax.ShapeDtypeStruct(query_key.shape, bf16),
            jax.ShapeDtypeStruct(values.shape, bf16),
            jax.ShapeDtypeStruct((rows_all, width), f32),
        ),
        in_specs=[
            pl.BlockSpec(memory_space=pltpu.SMEM),
            hbm,
            hbm,
            hbm,
            hbm,
            whole,
            whole,
            whole,
            whole,
            whole,
            whole,
        ],
        out_specs=(hbm, hbm, hbm),
        scratch_shapes=scratch,
        compiler_params=pltpu.CompilerParams(
            collective_id=0, has_side_effects=True, vmem_limit_bytes=67_043_328
        ),
    )(
        doc_lengths,
        query_key,
        values,
        out_grad,
        out_weight,
        jnp.asarray(LEFT, bf16),
        jnp.asarray(RIGHT, bf16),
        jnp.asarray(LEFT.T, bf16),
        jnp.asarray(RIGHT.T, bf16),
        jnp.asarray(COLS),
        jnp.asarray(np.broadcast_to(COLS[:, 3][None], (8, FEAT)).copy()),
    )
    return hand_on(*results)


def solution(mesh):
    placed = (P("ctx", "head"), P("ctx", "head"), P("ctx", "head"), P("head", None), P())
    return jax.shard_map(
        on_device,
        mesh=mesh,
        in_specs=placed,
        out_specs=(P("ctx", "head"), P("ctx", "head"), P("head", "ctx")),
        check_vma=False,
    )
```

time: 132 us -> 112 us (0.85)
  the two profiles are of different devices: /device:TPU:26 before, /device:TPU:16 now
where the time goes in v1:
time: 112 us
  Pallas kernels  111 us (99%)
    pallas_call x1, Pallas kernels, on_device(): pl.pallas_call(functools.partial(kernel, count, depth), name='step', out_...  108 us
    pallas_call x1, Pallas kernels, hand_on(): pl.pallas_call(functools.partial(hand_on_kernel, cuts), name='hand_on', o...  2.97 us

profile of v1, /device:TPU:16, one launch (start us, length us, event | category | flops | bytes accessed | tf_op | source)
XLA Modules:
  0.0 112.2 jit_solution(5115956354725236140)
XLA Ops:
  0.6 108.5 %step.1 = (bf16[512,256]{1,0:T(8,128)(2,1)}, bf16[512,1024]{1,0:T(8,128)(2,1)}, f32[1024,512]{1,0:T(8,128)}) custom-call(s32[32]{0:T(128)} %docs_ref.1, bf16[512,256]{1,0:T(8,128)(2,1)} %qk_hbm.1, bf16[512,1024]{1,0:T(8,128)(2,1)} %v_hbm.1, bf16[512,1024]{1,0:T(8,128)(2,1)} %g_ref.1, bf16[1024,4096]{1,0:T(8,128)(2,1)} %w_ref.1, ...), custom_call_target="tpu_custom_call" | custom-call | tf_op jit(solution)/shard_map/step/pallas_call | solution.py:892
  109.1 3.0 %hand_on.1 = (bf16[512,256]{1,0:T(8,128)(2,1)}, bf16[512,1024]{1,0:T(8,128)(2,1)}, f32[1024,512]{1,0:T(8,128)}) custom-call(bf16[512,256]{1,0:T(8,128)(2,1)} %get-tuple-element.6.refs_0_, bf16[512,1024]{1,0:T(8,128)(2,1)} %get-tuple-element.7.refs_1_, f32[1024,512]{1,0:T(8,128)} %get-tuple-element.8.refs_2_), custom_call_target="tpu_custom_call" | custom-call | tf_op jit(solution)/shard_map/hand_on/pallas_call | solution.py:811

commit v2 on v1

--- a/solution.py
+++ b/solution.py
@@ -485,13 +485,37 @@
             )
             y_ref[h, :, at] = mm(v_ref[:upto, head_rows(h)], weight_b, 0, 0)
 
+    row_block = min(256, rows_all)
+    blocks_of_rows = rows_all // row_block
+
+    def upstream(n, low, high):
+        if low == 0:
+            for copy in w_copies(n):
+                copy.wait()
+
+        @pl.loop(0, blocks_of_rows)
+        def _(b):
+            at = pl.ds(pl.multiple_of(b * row_block, row_block), row_block)
+            total = None if n == 0 and low == 0 else up_ref[at, :]
+            for g in range(low, high):
+                one = mm(wbuf[n % 2, g, at, :], out_ref[n, g], 1, 1)
+                total = one if total is None else total + one
+            up_ref[at, :] = total
+
+        if high == shares and n + 2 < depth:
+            start_all(w_copies(n + 2))
+
     each_head(0, heads // 4, attend)
     carry_pair(0)
     each_head(heads // 4, heads // 2, attend)
     arrive(1, 0)
-    each_head(heads // 2, 3 * heads // 4, attend)
+    each_head(heads // 2, heads, attend)
+    for copy in own_copies:
+        copy.wait()
+    upstream(0, 0, shares)
     carry_arrive(0)
-    each_head(3 * heads // 4, heads, attend)
+    if shares > 1:
+        arrive(1, 1)
     total_arrival(0).wait_recv()
 
     def finish_forward(h):
@@ -508,11 +532,6 @@
         att_ref[head_rows(h), :] = y.astype(bf16)
 
     each_head(0, heads, finish_forward)
-    for copy in own_copies:
-        copy.wait()
-
-    row_block = min(256, rows_all)
-    blocks_of_rows = rows_all // row_block
 
     def partner_copy(m):
         return pltpu.make_async_remote_copy(
@@ -527,37 +546,21 @@
     def product(m):
         n, g = m // shares, m % shares
 
-        @pl.loop(0, blocks_of_rows)
-        def _(b):
-            at = pl.ds(pl.multiple_of(b * row_block, row_block), row_block)
-            both_cores = mm(att_ref[at, :], out_ref[n, g], 1, 0)
-            for mine in range(2):
-
-                @pl.when(core == mine)
-                def _():
-                    for j in range(roots):
-                        to = slice(j * cg, (j + 1) * cg)
-                        theirs = (2 * j + 1 - mine) * cg
-                        ours = (2 * j + mine) * cg
-                        psend[m, at, to] = both_cores[:, theirs : theirs + cg].astype(bf16)
-                        acc[m, at, to] = both_cores[:, ours : ours + cg]
-
+        def halves(mine):
+            @pl.loop(0, blocks_of_rows)
+            def _(b):
+                at = pl.ds(pl.multiple_of(b * row_block, row_block), row_block)
+                both_cores = mm(att_ref[at, :], out_ref[n, g], 1, 0)
+                for j in range(roots):
+                    to = slice(j * cg, (j + 1) * cg)
+                    theirs = (2 * j + 1 - mine) * cg
+                    ours = (2 * j + mine) * cg
+                    psend[m, at, to] = both_cores[:, theirs : theirs + cg].astype(bf16)
+                    acc[m, at, to] = both_cores[:, ours : ours + cg]
+
+        for mine in range(2):
+            pl.when(core == mine)(lambda mine=mine: halves(mine))
         partner_copy(m).start()
-
-    def upstream(m):
-        n, g = m // shares, m % shares
-        if g == 0:
-            for copy in w_copies(n):
-                copy.wait()
-
-        @pl.loop(0, blocks_of_rows)
-        def _(b):
-            at = pl.ds(pl.multiple_of(b * row_block, row_block), row_block)
-            one = mm(wbuf[n % 2, g, at, :], out_ref[n, g], 1, 1)
-            up_ref[at, :] = one if m == 0 else up_ref[at, :] + one
-
-        if g == shares - 1 and n + 2 < depth:
-            start_all(w_copies(n + 2))
 
     if bits == 2:
         flows = [
@@ -653,14 +656,19 @@
     for m in range(last):
         if m >= 2 * shares:
             arrive(m // shares, m % shares)
-        if 0 < m < shares:
+        if 1 < m < shares:
             arrive(1, m)
         product(m)
-        upstream(m)
+        n, g = m // shares, m % shares
+        if n == depth - 1:
+            if g == shares - 2:
+                upstream(n, 0, shares - 1)
+        elif n > 0 and g == shares - 1:
+            upstream(n, 0, shares)
         trees(m)
     arrive(last // shares, last % shares)
     product(last)
-    upstream(last)
+    upstream(depth - 1, shares - 1, shares)
 
     def start_backward(h):
         up = up_ref[head_rows(h), :]
@@ -724,7 +732,7 @@
     for h in range(heads):
         each_head(h, h + 1, attention_grad)
         remaining(h)
-        if h == heads // 2:
+        if h == heads - 2:
             carry_arrive(1)
 
     total_arrival(1).wait_recv()

time: 112 us -> 110 us (0.982)
  Pallas kernels: 111 us -> 109 us
    pallas_call x1, Pallas kernels: 108 us -> 106 us  [on_device(): pl.pallas_call(functools.partial(kernel, count, depth), name='step', out_...]
where the time goes in v2:
time: 110 us; the launch traced here: 109 us
  Pallas kernels  109 us (99%)
    pallas_call x1, Pallas kernels, on_device(): pl.pallas_call(functools.partial(kernel, count, depth), name='step', out_...  106 us
    pallas_call x1, Pallas kernels, hand_on(): pl.pallas_call(functools.partial(hand_on_kernel, cuts), name='hand_on', o...  2.97 us

profile of v2, /device:TPU:16, one launch (start us, length us, event | category | flops | bytes accessed | tf_op | source)
XLA Modules:
  0.0 109.4 jit_solution(12313553636409208722)
XLA Ops:
  0.6 105.7 %step.1 = (bf16[512,256]{1,0:T(8,128)(2,1)}, bf16[512,1024]{1,0:T(8,128)(2,1)}, f32[1024,512]{1,0:T(8,128)}) custom-call(s32[32]{0:T(128)} %docs_ref.1, bf16[512,256]{1,0:T(8,128)(2,1)} %qk_hbm.1, bf16[512,1024]{1,0:T(8,128)(2,1)} %v_hbm.1, bf16[512,1024]{1,0:T(8,128)(2,1)} %g_ref.1, bf16[1024,4096]{1,0:T(8,128)(2,1)} %w_ref.1, ...), custom_call_target="tpu_custom_call" | custom-call | tf_op jit(solution)/shard_map/step/pallas_call | solution.py:900
  106.3 3.0 %hand_on.1 = (bf16[512,256]{1,0:T(8,128)(2,1)}, bf16[512,1024]{1,0:T(8,128)(2,1)}, f32[1024,512]{1,0:T(8,128)}) custom-call(bf16[512,256]{1,0:T(8,128)(2,1)} %get-tuple-element.6.refs_0_, bf16[512,1024]{1,0:T(8,128)(2,1)} %get-tuple-element.7.refs_1_, f32[1024,512]{1,0:T(8,128)} %get-tuple-element.8.refs_2_), custom_call_target="tpu_custom_call" | custom-call | tf_op jit(solution)/shard_map/hand_on/pallas_call | solution.py:819

commit v3 on v2

--- a/solution.py
+++ b/solution.py
@@ -723,7 +723,7 @@
         qkg[query_rows(h), :] += feature_grad(grad, first, second) * carried_row
 
     rounds = LAG * stages
-    steps = 2 * heads
+    steps = heads + 2
 
     def remaining(at):
         for r in range(at * rounds // steps, (at + 1) * rounds // steps):
@@ -732,7 +732,7 @@
     for h in range(heads):
         each_head(h, h + 1, attention_grad)
         remaining(h)
-        if h == heads - 2:
+        if h == heads - 1:
             carry_arrive(1)
 
     total_arrival(1).wait_recv()

time: 110 us -> 111 us (level)
  the two profiles are of different devices: /device:TPU:16 before, /device:TPU:24 now
where the time goes in v3:
time: 111 us
  Pallas kernels  110 us (99%)
    pallas_call x1, Pallas kernels, on_device(): pl.pallas_call(functools.partial(kernel, count, depth), name='step', out_...  107 us
    pallas_call x1, Pallas kernels, hand_on(): pl.pallas_call(functools.partial(hand_on_kernel, cuts), name='hand_on', o...  2.97 us

profile of v3, /device:TPU:24, one launch (start us, length us, event | category | flops | bytes accessed | tf_op | source)
XLA Modules:
  0.0 111.2 jit_solution(13134830086970636792)
XLA Ops:
  0.6 107.4 %step.1 = (bf16[512,256]{1,0:T(8,128)(2,1)}, bf16[512,1024]{1,0:T(8,128)(2,1)}, f32[1024,512]{1,0:T(8,128)}) custom-call(s32[32]{0:T(128)} %docs_ref.1, bf16[512,256]{1,0:T(8,128)(2,1)} %qk_hbm.1, bf16[512,1024]{1,0:T(8,128)(2,1)} %v_hbm.1, bf16[512,1024]{1,0:T(8,128)(2,1)} %g_ref.1, bf16[1024,4096]{1,0:T(8,128)(2,1)} %w_ref.1, ...), custom_call_target="tpu_custom_call" | custom-call | tf_op jit(solution)/shard_map/step/pallas_call | solution.py:900
  108.1 3.0 %hand_on.1 = (bf16[512,256]{1,0:T(8,128)(2,1)}, bf16[512,1024]{1,0:T(8,128)(2,1)}, f32[1024,512]{1,0:T(8,128)}) custom-call(bf16[512,256]{1,0:T(8,128)(2,1)} %get-tuple-element.6.refs_0_, bf16[512,1024]{1,0:T(8,128)(2,1)} %get-tuple-element.7.refs_1_, f32[1024,512]{1,0:T(8,128)} %get-tuple-element.8.refs_2_), custom_call_target="tpu_custom_call" | custom-call | tf_op jit(solution)/shard_map/hand_on/pallas_call | solution.py:819
